TPU v7x, 32 devices: a whole 2x2x4 slice. The times are simulated.
32 devices in a mesh: grp: 2 (over x), pix: 16 (over z, y, core).
Axes of the slice: x: 2, y: 2, z: 4, core: 2. Of those that a mesh axis runs over, the one named last changes fastest.
Arguments:
- particle_images: bfloat16 [8192, 128, 128], P(('grp', 'pix')), parts along dimension 0, may hold values from -6 to 6
- defocus_group: int32 [8192], P(('grp', 'pix')), parts along dimension 0, may hold values from 0 to 63
- live_counts: int32 [32], P(('grp', 'pix')), parts along dimension 0, may hold values from 192 to 256, as said below
- defocus_values: float32 [128], P('grp'), parts along dimension 0, may hold values from 50 to 400
- test_matrix: bfloat16 [32768, 128], P(('grp', 'pix')), parts along dimension 0, may hold values from -0.046875 to 0.046875
Outputs:
- range_basis: bfloat16 [8192, 128], P(('grp', 'pix')), parts along dimension 0
- projection: float32 [32768, 128], P(('grp', 'pix')), parts along dimension 0
There are 2 independent parts, one for each index of `grp`. A program takes and returns all parts, laid end to end along the dimension named above; each array names one. Nothing has to cross between parts.
Inputs may be any that keep to these rules, and one draw needn't show every extreme that they name: `live_counts`: each entry is the number of live particle slots of a shard, counted from its first slot; some shard is full in every draw.
All inputs are finite; a program needn't handle non-finite values.
Results may differ from a plain program's by a relative error of at most 0.011.
Values may be sent and summed in bfloat16 or wider, within the bound.
A program may use at most 192 MiB of HBM per device.

v0:
```python
import math

import jax
import jax.numpy as jnp
from jax import lax
from jax.sharding import PartitionSpec as P

AMPLITUDE = 0.1
WIENER = 0.1


def frequency_sq(length):
    indices = jnp.arange(length, dtype=jnp.int32)
    frequency = (
        jnp.where(indices < length // 2, indices, indices - length).astype(jnp.float32) / length
    )
    return frequency[:, None] ** 2 + frequency[None, :] ** 2


def wiener_table(defocus_values, length):
    phases = jnp.pi * defocus_values[:, None, None] * frequency_sq(length)[None]
    contrast = -(math.sqrt(1.0 - AMPLITUDE**2) * jnp.sin(phases) + AMPLITUDE * jnp.cos(phases))
    return contrast / (contrast * contrast + WIENER)


def dft_tables(length):
    indices = jnp.arange(length, dtype=jnp.int32)
    product = indices[:, None] * indices[None, :] % length
    angles = 2.0 * math.pi / length * product.astype(jnp.float32)
    return (jnp.cos(angles).astype(jnp.bfloat16), jnp.sin(angles).astype(jnp.bfloat16))


def left_apply(table_now, values_now):
    return jnp.einsum("uj,bjv->buv", table_now, values_now, preferred_element_type=jnp.float32)


def right_apply(values_now, table_now):
    return jnp.einsum("bjk,kv->bjv", values_now, table_now, preferred_element_type=jnp.float32)


def correct_block(images_blk, filter_now, cosine_table, sine_table):
    length = cosine_table.shape[0]
    both_tables = jnp.concatenate([cosine_table, sine_table], axis=1)
    first_pass = right_apply(images_blk, both_tables).astype(jnp.bfloat16)
    cos_side = left_apply(cosine_table, first_pass)
    sin_side = left_apply(sine_table, first_pass)
    filt_re = ((cos_side[..., :length] - sin_side[..., length:]) * filter_now).astype(jnp.bfloat16)
    filt_im = (-(cos_side[..., length:] + sin_side[..., :length]) * filter_now).astype(jnp.bfloat16)
    re_both = right_apply(filt_re, both_tables)
    im_both = right_apply(filt_im, both_tables)
    back_re = (re_both[..., :length] - im_both[..., length:]).astype(jnp.bfloat16)
    back_im = (re_both[..., length:] + im_both[..., :length]).astype(jnp.bfloat16)
    result_now = left_apply(cosine_table, back_re) - left_apply(sine_table, back_im)
    return result_now / float(length * length)


def per_device(particle_images, defocus_group, live_counts, defocus_values, test_matrix):
    part_rows = particle_images.shape[0]
    length = particle_images.shape[1]
    pixels = length * length
    groups_all = defocus_values.shape[0]
    filter_table = (
        wiener_table(defocus_values, length).reshape(groups_all, pixels).astype(jnp.bfloat16)
    )
    cosine_table, sine_table = dft_tables(length)
    group_hot = (defocus_group[:, None] == jnp.arange(groups_all, dtype=jnp.int32)[None, :]).astype(
        jnp.bfloat16
    )
    block_size = math.gcd(part_rows, 128)
    blocks = part_rows // block_size

    def correct(block_pair):
        images_blk, hot_blk = block_pair
        filter_now = jnp.dot(hot_blk, filter_table, preferred_element_type=jnp.float32).reshape(
            block_size, length, length
        )
        return correct_block(images_blk, filter_now, cosine_table, sine_table).reshape(
            block_size, pixels
        )

    corrected = lax.map(
        correct,
        (
            particle_images.reshape(blocks, block_size, length, length),
            group_hot.reshape(blocks, block_size, groups_all),
        ),
    )
    corrected = corrected.reshape(part_rows, pixels)
    live_rows = jnp.arange(part_rows, dtype=jnp.int32) < live_counts[0]
    corrected = jnp.where(live_rows[:, None], corrected, 0.0).astype(jnp.bfloat16)
    columns = corrected
    sketch = jnp.dot(
        columns,
        lax.all_gather(test_matrix, "pix", axis=0, tiled=True),
        preferred_element_type=jnp.float32,
    )
    local_gram = jnp.dot(sketch.T, sketch, precision=lax.Precision.HIGHEST)
    factor_low = jnp.linalg.cholesky(lax.psum(local_gram, "pix"))
    range_basis = lax.linalg.triangular_solve(
        factor_low, sketch, left_side=False, lower=True, transpose_a=True
    ).astype(jnp.bfloat16)
    columns = corrected
    projection = lax.psum_scatter(
        lax.dot_general(
            columns, range_basis, (((0,), (0,)), ((), ())), preferred_element_type=jnp.float32
        ),
        "pix",
        scatter_dimension=0,
        tiled=True,
    )
    return (range_basis, projection)


def solution(mesh):
    placed = (
        P(("grp", "pix"), None, None),
        P(("grp", "pix")),
        P(("grp", "pix")),
        P("grp"),
        P(("grp", "pix"), None),
    )
    return jax.shard_map(
        per_device,
        mesh=mesh,
        in_specs=placed,
        out_specs=(P(("grp", "pix"), None), P(("grp", "pix"), None)),
        check_vma=False,
    )
```

profile of v0, /device:TPU:0, one launch (start us, length us, event | category | flops | bytes accessed | tf_op | source)
XLA Modules:
  0.0 487.4 jit_solution(18269629474822703889)
XLA Ops:
  7.2 0.0 all-gather.2.cloned.1.call-start
  7.2 0.7 all-gather.2.cloned.1.call-update
  7.9 0.0 all-reduce.2.cloned.1.call-start
  7.9 0.3 sine_convert_fusion.1
  8.2 0.2 add.82
  8.5 0.7 fusion.82
  9.2 0.7 broadcast_multiply_fusion
  9.8 226.4 %while.13 = (s32[]{:T(128)}, bf16[2,128,16384]{2,1,0:T(8,128)(2,1)}, bf16[2,128,128,128]{3,2,1,0:T(8,128)(2,1)}, bf16[128,256]{1,0:T(8,128)(2,1)S(1)}, bf16[2,12...) while((s32[]{:T(128)}, ...), condition=%wide.region_1.2_spmd.clone.clone, body=%wide.region_0.1_spmd.clone.clone.sunk | while | flops 6754861056 | bytes 285492864 | solution.py:81
  9.8 4.5 convolution_convert_fusion.3
  14.4 7.5 %convolution_bitcast_fusion.4 = f32[128,128,256]{1,2,0:T(8,128)} fusion(bf16[128,128,256]{2,1,0:T(8,128)(2,1)S(1)} %convolution_convert_fusion.3), kind=kOutput, calls=%fused_computation.3.clone.1 | convolution fusion | flops 1073987584 | bytes 25165824 | tf_op jit(solution)/shard_map/while/body/eval_jaxpr/uj,bjv->buv/dot_general | solution.py:34
  21.9 7.3 %convolution_bitcast_fusion.5 = f32[128,128,256]{1,2,0:T(8,128)} fusion(bf16[128,128,256]{2,1,0:T(8,128)(2,1)S(1)} %convolution_convert_fusion.3), kind=kOutput, calls=%fused_computation.4.clone.1 | convolution fusion | flops 1073987584 | bytes 25165824 | tf_op jit(solution)/shard_map/while/body/eval_jaxpr/uj,bjv->buv/dot_general | solution.py:34
  29.1 18.8 %fusion.138 = f32[128,128,128]{2,0,1:T(8,128)} fusion(bf16[2,128,64]{1,2,0:T(8,128)(2,1)S(1)} %get-tuple-element.202, s32[]{:T(128)} %get-tuple-element.190, f32[16384]{0:T(1024)S(1)} %get-tuple-element.203, f32[64]{0:T(128)S(1)} %get-tuple-element.204), kind=kOutput, calls=%fused_computation.35.clone.1 | convolution fusion | flops 277872640 | bytes 8471044 | tf_op jit(solution)/shard_map/while/body/eval_jaxpr/dot_general | solution.py:74
  48.0 9.4 %copy.62 = f32[128,128,128]{1,2,0:T(8,128)} copy(f32[128,128,128]{2,0,1:T(8,128)} %fusion.138) | data formatting | bytes 16777216 | tf_op jit(solution)/shard_map/while/body/eval_jaxpr/dot_general | solution.py:74
  57.3 0.0 copy-start
  57.3 16.7 %fusion.140 = f32[128,128,256]{2,1,0:T(8,128)} fusion(f32[128,128,128]{1,2,0:T(8,128)} %copy.62, f32[128,128,256]{1,2,0:T(8,128)} %convolution_bitcast_fusion.4, f32[128,128,256]{1,2,0:T(8,128)} %convolution_bitcast_fusion.5, bf16[128,256]{1,0:T(8,128)(2,1)S(1)} %get-tuple-element.201), kind=kOutput, calls=%fused_computation.28.clone.1 | convolution fusion | flops 1080033280 | bytes 42008576 | tf_op jit(solution)/shard_map/while/body/eval_jaxpr/bjk,kv->bjv/dot_general | solution.py:38
  74.0 0.0 copy-done
  74.0 14.0 %fusion.139 = f32[128,128,256]{2,1,0:T(8,128)} fusion(f32[128,128,128]{1,2,0:T(8,128)S(1)} %copy-done, f32[128,128,256]{1,2,0:T(8,128)} %convolution_bitcast_fusion.4, f32[128,128,256]{1,2,0:T(8,128)} %convolution_bitcast_fusion.5, bf16[128,256]{1,0:T(8,128)(2,1)S(1)} %get-tuple-element.201), kind=kOutput, calls=%fused_computation.29.clone.1 | convolution fusion | flops 1082130432 | bytes 42008576 | tf_op jit(solution)/shard_map/while/body/eval_jaxpr/bjk,kv->bjv/dot_general | solution.py:38
  88.0 7.5 %fusion.141 = f32[128,128,128]{2,1,0:T(8,128)S(1)} fusion(f32[128,128,256]{2,1,0:T(8,128)} %fusion.139, f32[128,128,256]{2,1,0:T(8,128)} %fusion.140), kind=kOutput, calls=%fused_computation.30.clone.1 | convolution fusion | flops 541310976 | bytes 25165824 | tf_op jit(solution)/shard_map/while/body/eval_jaxpr/uj,bjv->buv/dot_general | solution.py:34
  95.5 9.7 %multiply_bitcast_fusion.2 = bf16[128,128,128]{1,2,0:T(8,128)(2,1)} fusion(f32[128,128,128]{2,1,0:T(8,128)S(1)} %fusion.141, f32[128,128,256]{2,1,0:T(8,128)} %fusion.139, f32[128,128,256]{2,1,0:T(8,128)} %fusion.140), kind=kOutput, calls=%fused_computation.16.clone.1 | convolution fusion | flops 547602432 | bytes 29360128 | tf_op jit(solution)/shard_map/while/body/eval_jaxpr/uj,bjv->buv/dot_general | solution.py:34
  105.2 7.3 %copy.63 = bf16[128,128,128]{0,2,1:T(8,128)(2,1)} copy(bf16[128,128,128]{1,2,0:T(8,128)(2,1)} %multiply_bitcast_fusion.2) | data formatting | bytes 8388608 | tf_op jit(solution)/shard_map/while/body/eval_jaxpr/div | solution.py:54
  112.5 6.4 %copy.64 = bf16[1,128,16384]{2,1,0:T(8,128)(2,1)} copy(bf16[1,128,16384]{1,2,0:T(8,128)(2,1)} %bitcast.100) | data formatting | bytes 8388608 | tf_op jit(solution)/shard_map/while/body/jit(dynamic_update_index_in_dim)/dynamic_update_slice | solution.py:81
  118.8 4.5 constant_dynamic-update-slice_fusion.2
  123.4 4.5 convolution_convert_fusion.3
  127.9 7.3 %convolution_bitcast_fusion.4 = f32[128,128,256]{1,2,0:T(8,128)} fusion(bf16[128,128,256]{2,1,0:T(8,128)(2,1)S(1)} %convolution_convert_fusion.3), kind=kOutput, calls=%fused_computation.3.clone.1 | convolution fusion | flops 1073987584 | bytes 25165824 | tf_op jit(solution)/shard_map/while/body/eval_jaxpr/uj,bjv->buv/dot_general | solution.py:34
  135.1 7.2 %convolution_bitcast_fusion.5 = f32[128,128,256]{1,2,0:T(8,128)} fusion(bf16[128,128,256]{2,1,0:T(8,128)(2,1)S(1)} %convolution_convert_fusion.3), kind=kOutput, calls=%fused_computation.4.clone.1 | convolution fusion | flops 1073987584 | bytes 25165824 | tf_op jit(solution)/shard_map/while/body/eval_jaxpr/uj,bjv->buv/dot_general | solution.py:34
  142.4 18.8 %fusion.138 = f32[128,128,128]{2,0,1:T(8,128)} fusion(bf16[2,128,64]{1,2,0:T(8,128)(2,1)S(1)} %get-tuple-element.202, s32[]{:T(128)} %get-tuple-element.190, f32[16384]{0:T(1024)S(1)} %get-tuple-element.203, f32[64]{0:T(128)S(1)} %get-tuple-element.204), kind=kOutput, calls=%fused_computation.35.clone.1 | convolution fusion | flops 277872640 | bytes 8471044 | tf_op jit(solution)/shard_map/while/body/eval_jaxpr/dot_general | solution.py:74
  161.2 9.3 %copy.62 = f32[128,128,128]{1,2,0:T(8,128)} copy(f32[128,128,128]{2,0,1:T(8,128)} %fusion.138) | data formatting | bytes 16777216 | tf_op jit(solution)/shard_map/while/body/eval_jaxpr/dot_general | solution.py:74
  170.5 0.0 copy-start
  170.5 16.4 %fusion.140 = f32[128,128,256]{2,1,0:T(8,128)} fusion(f32[128,128,128]{1,2,0:T(8,128)} %copy.62, f32[128,128,256]{1,2,0:T(8,128)} %convolution_bitcast_fusion.4, f32[128,128,256]{1,2,0:T(8,128)} %convolution_bitcast_fusion.5, bf16[128,256]{1,0:T(8,128)(2,1)S(1)} %get-tuple-element.201), kind=kOutput, calls=%fused_computation.28.clone.1 | convolution fusion | flops 1080033280 | bytes 42008576 | tf_op jit(solution)/shard_map/while/body/eval_jaxpr/bjk,kv->bjv/dot_general | solution.py:38
  186.9 0.0 copy-done
  186.9 14.0 %fusion.139 = f32[128,128,256]{2,1,0:T(8,128)} fusion(f32[128,128,128]{1,2,0:T(8,128)S(1)} %copy-done, f32[128,128,256]{1,2,0:T(8,128)} %convolution_bitcast_fusion.4, f32[128,128,256]{1,2,0:T(8,128)} %convolution_bitcast_fusion.5, bf16[128,256]{1,0:T(8,128)(2,1)S(1)} %get-tuple-element.201), kind=kOutput, calls=%fused_computation.29.clone.1 | convolution fusion | flops 1082130432 | bytes 42008576 | tf_op jit(solution)/shard_map/while/body/eval_jaxpr/bjk,kv->bjv/dot_general | solution.py:38
  200.9 7.5 %fusion.141 = f32[128,128,128]{2,1,0:T(8,128)S(1)} fusion(f32[128,128,256]{2,1,0:T(8,128)} %fusion.139, f32[128,128,256]{2,1,0:T(8,128)} %fusion.140), kind=kOutput, calls=%fused_computation.30.clone.1 | convolution fusion | flops 541310976 | bytes 25165824 | tf_op jit(solution)/shard_map/while/body/eval_jaxpr/uj,bjv->buv/dot_general | solution.py:34
  208.4 9.7 %multiply_bitcast_fusion.2 = bf16[128,128,128]{1,2,0:T(8,128)(2,1)} fusion(f32[128,128,128]{2,1,0:T(8,128)S(1)} %fusion.141, f32[128,128,256]{2,1,0:T(8,128)} %fusion.139, f32[128,128,256]{2,1,0:T(8,128)} %fusion.140), kind=kOutput, calls=%fused_computation.16.clone.1 | convolution fusion | flops 547602432 | bytes 29360128 | tf_op jit(solution)/shard_map/while/body/eval_jaxpr/uj,bjv->buv/dot_general | solution.py:34
  218.1 7.3 %copy.63 = bf16[128,128,128]{0,2,1:T(8,128)(2,1)} copy(bf16[128,128,128]{1,2,0:T(8,128)(2,1)} %multiply_bitcast_fusion.2) | data formatting | bytes 8388608 | tf_op jit(solution)/shard_map/while/body/eval_jaxpr/div | solution.py:54
  225.3 6.4 %copy.64 = bf16[1,128,16384]{2,1,0:T(8,128)(2,1)} copy(bf16[1,128,16384]{1,2,0:T(8,128)(2,1)} %bitcast.100) | data formatting | bytes 8388608 | tf_op jit(solution)/shard_map/while/body/jit(dynamic_update_index_in_dim)/dynamic_update_slice | solution.py:81
  231.7 4.5 constant_dynamic-update-slice_fusion.2
  236.9 8.6 %fusion.72 = bf16[256,16384]{1,0:T(8,128)(2,1)} fusion(bf16[2,128,16384]{2,1,0:T(8,128)(2,1)} %get-tuple-element.79, pred[256]{0:T(512)(128)(4,1)S(1)} %iota_compare_fusion.3), kind=kLoop, calls=%fused_computation.76 | loop fusion | flops 4194304 | bytes 16777472 | tf_op jit(solution)/shard_map/convert_element_type | solution.py:90
  245.4 0.0 all-gather.2.cloned.1.call-done
  245.4 6.9 %fusion.86 = f32[256,128]{1,0:T(8,128)S(1)} fusion(bf16[256,16384]{1,0:T(8,128)(2,1)} %fusion.72, bf16[16384,128]{1,0:T(8,128)(2,1)} %all-gather.2.cloned.1.call-done), kind=kOutput, calls=%fused_computation.108 | convolution fusion | flops 1073741824 | bytes 12713984 | tf_op jit(solution)/shard_map/dot_general | solution.py:92
  252.4 1.0 fusion.87
  253.4 0.0 all-reduce.2.cloned.1.call-update
  253.4 0.0 reduce-scatter.2.cloned.1.call-start
  253.4 87.1 %all-reduce.2.cloned.1.call-done = f32[128,128]{0,1:T(8,128)} async-done(((f32[128,128]{0,1:T(8,128)}), f32[128,128]{0,1:T(8,128)}) %all-reduce.2.cloned.1.call-update) | async-done | bytes 65552 | tf_op jit(solution)/shard_map/psum | solution.py:98
  340.6 0.9 copy.41
  341.5 0.9 fusion.78
  342.3 11.7 %cholesky.16 = f32[128,128]{1,0:T(8,128)S(1)} custom-call(f32[128,128]{1,0:T(8,128)S(1)} %fusion.78), custom_call_target="Cholesky" | custom-call | tf_op jit(solution)/shard_map/jit(cholesky)/cholesky | solution.py:98
  354.1 0.6 compare_reduce_fusion
  354.7 0.7 fusion.73
  355.4 9.8 %custom-call.6 = f32[1,128,128]{1,2,0:T(8,128)S(1)} custom-call(f32[1,128,128]{2,1,0:T(8,128)S(1)} %fusion.73), custom_call_target="InvertDiagBlocksLowerTriangular" | custom-call | tf_op jit(solution)/shard_map/triangular_solve | solution.py:99
  365.2 0.3 convolution_convert_fusion.1
  365.5 0.0 copy-start.1
  365.5 9.0 %fusion.88 = f32[16384,128]{1,0:T(8,128)} fusion(bf16[256,16384]{1,0:T(8,128)(2,1)} %fusion.72, bf16[256,128]{1,0:T(8,128)(2,1)S(1)} %convolution_convert_fusion.1), kind=kOutput, calls=%fused_computation.110 | convolution fusion | flops 1073741824 | bytes 16842752 | tf_op jit(solution)/shard_map/dot_general | solution.py:104
  374.5 0.0 copy-done.1
  374.5 0.0 reduce-scatter.2.cloned.1.call-update
  374.6 106.3 %reduce-scatter.2.cloned.1.call-done = f32[1024,128]{1,0:T(8,128)} async-done(((f32[16384,128]{1,0:T(8,128)}), f32[1024,128]{1,0:T(8,128)}) %reduce-scatter.2.cloned.1.call-update) | async-done | bytes 524304 | tf_op jit(solution)/shard_map/reduce_scatter | solution.py:103
  (6 shorter events, 0.1 us)
Async XLA Ops:
  7.2 238.3 %all-gather.2.cloned.1.call-start = ((), (), s32[]{:S(2)}) async-start(), calls=%async_computation.1 | async-start | bytes 4456448 | tf_op jit(solution)/shard_map/all_gather | solution.py:94
  7.9 332.7 %all-reduce.2.cloned.1.call-start = ((), (), s32[]{:S(2)}) async-start(), calls=%async_computation.2 | async-start | bytes 131072 | tf_op jit(solution)/shard_map/psum | solution.py:98
  57.3 16.7 %copy-start = (f32[128,128,128]{1,2,0:T(8,128)S(1)}, f32[128,128,128]{1,2,0:T(8,128)}, u32[]{:S(2)}) copy-start(f32[128,128,128]{1,2,0:T(8,128)} %copy.62) | copy-start | bytes 25165828 | tf_op jit(solution)/shard_map/while
  170.5 16.4 %copy-start = (f32[128,128,128]{1,2,0:T(8,128)S(1)}, f32[128,128,128]{1,2,0:T(8,128)}, u32[]{:S(2)}) copy-start(f32[128,128,128]{1,2,0:T(8,128)} %copy.62) | copy-start | bytes 25165828 | tf_op jit(solution)/shard_map/while
  253.4 227.5 %reduce-scatter.2.cloned.1.call-start = ((), (), s32[]{:S(2)}) async-start(), calls=%async_computation.3 | async-start | bytes 8912896 | tf_op jit(solution)/shard_map/reduce_scatter | solution.py:103
  365.5 9.1 %copy-start.1 = (bf16[256,128]{1,0:T(8,128)(2,1)}, bf16[256,128]{1,0:T(8,128)(2,1)S(1)}, u32[]{:S(2)}) copy-start(bf16[256,128]{1,0:T(8,128)(2,1)S(1)} %convolution_convert_fusion.1) | copy-start | bytes 196612
Sparse Core Ops, SparseCore 0:
  10.2 53.3 all-gather.1
  253.5 86.9 all-reduce.1
  374.7 106.1 reduce-scatter.1
where the time goes:
time: 489 us; the launch traced here: 487 us
  waiting for transfers between devices  194 us (40%)
  matrix products  189 us (39%)
  local copies, waits for them, and re-layouts  56.1 us (11%)
  other arithmetic  34 us (7%)
  between operations  14.5 us (3%)
    reduce_scatter x1, waiting for transfers between devices, per_device(): lax.psum_scatter(lax.dot_general(columns, range_basis, (((0,), (0,)), (()...  106 us
    psum x1, waiting for transfers between devices, per_device(): factor_low = jnp.linalg.cholesky(lax.psum(local_gram, 'pix'))  87.1 us
    dot_general x6, matrix products, right_apply(): jnp.einsum('bjk,kv->bjv', values_now, table_now, preferred_element_type=j...  70.1 us
    dot_general x8, matrix products, left_apply(): jnp.einsum('uj,bjv->buv', table_now, values_now, preferred_element_type=j...  63.6 us
    dot_general x2, matrix products, correct(): jnp.dot(hot_blk, filter_table, preferred_element_type=jnp.float32)  37.7 us
    dynamic_update_slice x4, local copies, waits for them, and re-layouts, per_device(): lax.map(correct, (particle_images.reshape(blocks, block_size, length, len...  21.7 us
    dot_general x2, local copies, waits for them, and re-layouts, correct(): jnp.dot(hot_blk, filter_table, preferred_element_type=jnp.float32)  18.6 us
    div x2, local copies, waits for them, and re-layouts, correct_block(): return result_now / float(length * length)  14.5 us
  transfers between devices with their start and end apart: 3, of which 2 were waited for; matrix products, arithmetic and copies ran while one was open for 49% of the time, Pallas kernels for 0%

commit v1 on v0

v1 whole, which is shorter than its diff:
```python
import functools
import math

import jax
import jax.numpy as jnp
from jax import lax
from jax.experimental import pallas as pl
from jax.experimental.pallas import tpu as pltpu
from jax.sharding import PartitionSpec as P

AMPLITUDE = 0.1
WIENER = 0.1
F32 = jnp.float32
BF16 = jnp.bfloat16
HIGHEST = lax.Precision.HIGHEST


def real_tables(length):
    rows = jnp.arange(length, dtype=jnp.int32)
    product = rows[:, None] * rows[None, :] % length
    angles = 2.0 * math.pi / length * product.astype(F32)
    packed = jnp.where(rows[None, :] <= length // 2, jnp.cos(angles), jnp.sin(angles))
    return packed.astype(BF16)


def phase_tables(defocus_values, length):
    index = jnp.arange(length, dtype=jnp.int32)
    freq = jnp.where(index < length // 2, index, index - length).astype(F32) / length
    phase = jnp.pi * defocus_values[:, None] * (freq * freq)[None, :]
    sine, cosine = jnp.sin(phase), jnp.cos(phase)
    keep = math.sqrt(1.0 - AMPLITUDE**2)
    first = -(keep * sine + AMPLITUDE * cosine)
    second = -(keep * cosine - AMPLITUDE * sine)
    return cosine, sine, first, second


def correct_kernel(
    group_ref,
    live_ref,
    image_ref,
    row_cos_ref,
    row_sin_ref,
    first_ref,
    second_ref,
    pair_ref,
    pair_t_ref,
    table_ref,
    table_t_ref,
    weight_ref,
    out_ref,
    filters,
    turned,
):
    step = pl.program_id(0)
    count, length, _ = image_ref.shape
    groups = filters.shape[0]

    @pl.when(step == 0)
    def _():
        def fill(group, carry):
            contrast = (
                first_ref[group] * row_cos_ref[pl.ds(group, 1), :]
                + second_ref[group] * row_sin_ref[pl.ds(group, 1), :]
            )
            wiener = contrast / (contrast * contrast + WIENER)
            filters[group] = wiener.astype(BF16).astype(F32) * weight_ref[...]
            return carry

        lax.fori_loop(0, groups, fill, 0)

    for pair in range(count // 2):
        images = jnp.concatenate([image_ref[2 * pair], image_ref[2 * pair + 1]], axis=1)
        weights = jnp.concatenate(
            [
                filters[group_ref[step * count + 2 * pair]],
                filters[group_ref[step * count + 2 * pair + 1]],
            ],
            axis=1,
        )
        rows = jnp.dot(images, pair_ref[...], preferred_element_type=F32).astype(BF16)
        spectrum = jnp.dot(table_t_ref[...], rows, preferred_element_type=F32)
        kept = (spectrum * weights).astype(BF16)
        back = jnp.dot(kept, pair_t_ref[...], preferred_element_type=F32).astype(BF16)
        result = jnp.dot(table_ref[...], back, preferred_element_type=F32)
        for half in range(2):
            turned[pl.ds(2 * pair + half, length, stride=count), :] = result[
                :, half * length : (half + 1) * length
            ]
    slot = step * count + lax.broadcasted_iota(jnp.int32, (1, count, 1), 1)
    values = turned[...].reshape(length, count, length)
    out_ref[...] = jnp.where(slot < live_ref[0], values, 0.0).astype(BF16)


def correct(images, groups, live, defocus_values):
    slots, length, _ = images.shape
    count = math.gcd(slots, 16)
    table = real_tables(length)
    zero = jnp.zeros_like(table)
    pair = jnp.concatenate(
        [jnp.concatenate([table, zero], axis=1), jnp.concatenate([zero, table], axis=1)], axis=0
    )
    cosine, sine, first, second = phase_tables(defocus_values, length)
    index = jnp.arange(length, dtype=jnp.int32)
    twice = jnp.where((index == 0) | (index == length // 2), 1.0, 2.0).astype(F32)
    weight = twice[:, None] * twice[None, :] / float(length * length)
    number = defocus_values.shape[0]

    def whole(*shape):
        return pl.BlockSpec(shape, lambda i, *_: (0,) * len(shape))

    return pl.pallas_call(
        correct_kernel,
        out_shape=jax.ShapeDtypeStruct((length, slots, length), BF16),
        grid_spec=pltpu.PrefetchScalarGridSpec(
            num_scalar_prefetch=2,
            grid=(slots // count,),
            in_specs=[
                pl.BlockSpec((count, length, length), lambda i, *_: (i, 0, 0)),
                whole(number, length),
                whole(number, length),
                whole(number, length, 1),
                whole(number, length, 1),
                whole(2 * length, 2 * length),
                whole(2 * length, 2 * length),
                whole(length, length),
                whole(length, length),
                whole(length, length),
            ],
            out_specs=pl.BlockSpec((length, count, length), lambda i, *_: (0, i, 0)),
            scratch_shapes=[
                pltpu.VMEM((number, length, length), F32),
                pltpu.VMEM((length * count, length), F32),
            ],
        ),
        compiler_params=pltpu.CompilerParams(vmem_limit_bytes=48 << 20),
        cost_estimate=pl.CostEstimate(
            flops=16 * slots * length**3, bytes_accessed=4 * slots * length**2, transcendentals=0
        ),
        name="correct",
    )(
        groups,
        live,
        images,
        cosine,
        sine,
        first[:, :, None],
        second[:, :, None],
        pair,
        pair.T,
        table,
        table.T,
        weight,
    )


def sketch_kernel(column_ref, matrix_ref, sketch_ref):
    @pl.when(pl.program_id(0) == 0)
    def _():
        sketch_ref[...] = jnp.zeros_like(sketch_ref)

    count, _, length = column_ref.shape
    total = sketch_ref[...]
    for pair in range(count // 2):
        left = jnp.concatenate([column_ref[2 * pair], column_ref[2 * pair + 1]], axis=1)
        right = matrix_ref[pl.ds(2 * pair * length, 2 * length), :]
        total += jnp.dot(left, right, preferred_element_type=F32)
    sketch_ref[...] = total


def make_sketch(columns, matrix):
    length, slots, _ = columns.shape
    rank = matrix.shape[1]
    count = math.gcd(length, 16)
    return pl.pallas_call(
        sketch_kernel,
        out_shape=jax.ShapeDtypeStruct((slots, rank), F32),
        grid=(length // count,),
        in_specs=[
            pl.BlockSpec((count, slots, length), lambda i: (i, 0, 0)),
            pl.BlockSpec((count * length, rank), lambda i: (i, 0)),
        ],
        out_specs=pl.BlockSpec((slots, rank), lambda i: (0, 0)),
        compiler_params=pltpu.CompilerParams(vmem_limit_bytes=48 << 20),
        name="sketch",
    )(columns, matrix)


def project_kernel(column_ref, sketch_ref, out_ref, halves):
    rank = sketch_ref.shape[1]

    @pl.when(pl.program_id(0) == 0)
    def _():
        high = sketch_ref[...].astype(BF16)
        halves[:, :rank] = high
        halves[:, rank:] = (sketch_ref[...] - high.astype(F32)).astype(BF16)

    count, _, length = column_ref.shape
    for row in range(count):
        both = lax.dot_general(
            column_ref[row], halves[...], (((0,), (0,)), ((), ())), preferred_element_type=F32
        )
        out_ref[pl.ds(row * length, length), :] = both[:, :rank] + both[:, rank:]


def project(columns, sketch):
    length, slots, _ = columns.shape
    rank = sketch.shape[1]
    count = math.gcd(length, 8)
    return pl.pallas_call(
        project_kernel,
        out_shape=jax.ShapeDtypeStruct((length * length, rank), F32),
        grid=(length // count,),
        in_specs=[
            pl.BlockSpec((count, slots, length), lambda i: (i, 0, 0)),
            pl.BlockSpec((slots, rank), lambda i: (0, 0)),
        ],
        out_specs=pl.BlockSpec((count * length, rank), lambda i: (i, 0)),
        scratch_shapes=[pltpu.VMEM((slots, 2 * rank), BF16)],
        compiler_params=pltpu.CompilerParams(vmem_limit_bytes=48 << 20),
        name="project",
    )(columns, sketch)


def per_device(particle_images, defocus_group, live_counts, defocus_values, test_matrix):
    matrix = lax.all_gather(test_matrix, "pix", axis=0, tiled=True)
    columns = correct(particle_images, defocus_group, live_counts, defocus_values)
    sketch = make_sketch(columns, matrix)
    gram = lax.psum(jnp.dot(sketch.T, sketch, precision=HIGHEST), "pix")
    summed = lax.psum_scatter(project(columns, sketch), "pix", scatter_dimension=0, tiled=True)
    factor_low = jnp.linalg.cholesky(gram)
    rank = gram.shape[0]
    inverse_t = lax.linalg.triangular_solve(
        factor_low, jnp.eye(rank, dtype=F32), left_side=False, lower=True, transpose_a=True
    )
    range_basis = jnp.dot(sketch, inverse_t, precision=HIGHEST).astype(BF16)
    projection = jnp.dot(summed, inverse_t, precision=HIGHEST)
    return (range_basis, projection)


def solution(mesh):
    placed = (
        P(("grp", "pix"), None, None),
        P(("grp", "pix")),
        P(("grp", "pix")),
        P("grp"),
        P(("grp", "pix"), None),
    )
    return jax.shard_map(
        per_device,
        mesh=mesh,
        in_specs=placed,
        out_specs=(P(("grp", "pix"), None), P(("grp", "pix"), None)),
        check_vma=False,
    )
```

time: 489 us -> 303 us (0.62)
  matrix products: 189 us -> 4.49 us
  Pallas kernels: 0 us -> 79.3 us
  local copies, waits for them, and re-layouts: 56.1 us -> 3.22 us
  waiting for transfers between devices: 194 us -> 159 us
  other arithmetic: 34 us -> 41.9 us
    dot_general x19 -> x3, matrix products: 188 us -> 4.3 us  [the longest x1 2.4 us: per_device(): projection = jnp.dot(summed, inverse_t, precision=HIGHEST)]
    pallas_call x0 -> x3, Pallas kernels: none -> 79.3 us  [the longest x1 57.8 us: correct(): pl.pallas_call(correct_kernel, out_shape=jax.ShapeDtypeStruct((length, sl...]
    dynamic_update_slice x4 -> x0, local copies, waits for them, and re-layouts: 21.7 us -> none  [per_device(): lax.map(correct, (particle_images.reshape(blocks, block_size, length, len...]
    reduce_scatter x1, waiting for transfers between devices: 106 us -> 85.3 us  [per_device(): lax.psum_scatter(project(columns, sketch), 'pix', scatter_dimension=0, ti...]
    dot_general x2 -> x0, local copies, waits for them, and re-layouts: 18.6 us -> none  [correct(): jnp.dot(hot_blk, filter_table, preferred_element_type=jnp.float32)]
    neg x0 -> x1, other arithmetic: none -> 16.9 us  [phase_tables(): second = -(keep * cosine - AMPLITUDE * sine)]
    div x2 -> x0, local copies, waits for them, and re-layouts: 14.5 us -> none  [correct_block(): return result_now / float(length * length)]
    psum x1, waiting for transfers between devices: 87.1 us -> 72.8 us  [per_device(): gram = lax.psum(jnp.dot(sketch.T, sketch, precision=HIGHEST), 'pix')]
  transfers between devices with their start and end apart: 3 -> 3, of which waited for: 2 -> 2; matrix products, arithmetic and copies ran while one was open for 49% -> 15% of each run, Pallas kernels for 0% -> 24%
where the time goes in v1:
time: 303 us
  waiting for transfers between devices  159 us (52%)
  Pallas kernels  79.3 us (26%)
  other arithmetic  41.9 us (14%)
  between operations  14.5 us (5%)
  matrix products  4.49 us (1%)
  local copies, waits for them, and re-layouts  3.22 us (1%)
    reduce_scatter x1, waiting for transfers between devices, per_device(): lax.psum_scatter(project(columns, sketch), 'pix', scatter_dimension=0, ti...  85.3 us
    psum x1, waiting for transfers between devices, per_device(): gram = lax.psum(jnp.dot(sketch.T, sketch, precision=HIGHEST), 'pix')  72.8 us
    pallas_call x1, Pallas kernels, correct(): pl.pallas_call(correct_kernel, out_shape=jax.ShapeDtypeStruct((length, sl...  57.8 us
    neg x1, other arithmetic, phase_tables(): second = -(keep * cosine - AMPLITUDE * sine)  16.9 us
    pallas_call x1, Pallas kernels, project(): pl.pallas_call(project_kernel, out_shape=jax.ShapeDtypeStruct((length * l...  14.3 us
    another operation x3, other arithmetic, per_device(): factor_low = jnp.linalg.cholesky(gram)  12.4 us
    another operation x2, other arithmetic, per_device(): lax.linalg.triangular_solve(factor_low, jnp.eye(rank, dtype=F32), left_si...  10.5 us
    pallas_call x1, Pallas kernels, make_sketch(): pl.pallas_call(sketch_kernel, out_shape=jax.ShapeDtypeStruct((slots, rank...  7.3 us
  transfers between devices with their start and end apart: 3, of which 2 were waited for; matrix products, arithmetic and copies ran while one was open for 15% of the time, Pallas kernels for 24%

profile of v1, /device:TPU:0, one launch (start us, length us, event | category | flops | bytes accessed | tf_op | source)
XLA Modules:
  0.0 302.5 jit_solution(1834242174154411353)
XLA Ops:
  7.2 0.0 all-gather.2.cloned.1.call-start
  7.2 0.7 all-gather.2.cloned.1.call-update
  7.9 0.0 all-reduce.4.cloned.1.call-start
  8.0 0.3 select_convert_fusion
  8.3 0.1 copy.11.pair_t_ref
  9.1 0.7 broadcast_multiply_fusion
  9.7 0.1 multiply_multiply_fusion.weight_ref
  9.8 0.2 multiply_sine_fusion.1
  10.0 0.0 copy-start.1
  10.0 16.9 %fusion.7 = (f32[64,128,1]{2,1,0:T(8,128)}, f32[64,128,1]{2,1,0:T(8,128)S(1)}) fusion(f32[64]{0:T(128)S(1)} %broadcast_multiply_fusion, f32[128]{0:T(128)S(1)} %fusion.25), kind=kLoop, calls=%fused_computation.9 | loop fusion | flops 73728 | bytes 66304 | tf_op jit(solution)/shard_map/neg | solution.py:33
  26.9 0.0 copy-done.1
  26.9 57.8 %correct.1.column_ref = bf16[128,256,128]{2,1,0:T(8,128)(2,1)} custom-call(s32[256]{0:T(256)S(1)} %copy-done.1, s32[1]{0:T(128)S(6)} %copy.16.live_ref, bf16[256,128,128]{2,1,0:T(8,128)(2,1)} %image_ref.1, f32[64,128]{1,0:T(8,128)S(1)} %get-tuple-element.7.row_cos_ref, f32[64,128]{1,0:T(8,128)S(1)} %get-tuple-element.6.row_sin_ref, ...), custom_call_target="tpu_custom_call" | custom-call | flops 8589934592 | bytes 16777216 | tf_op jit(solution)/shard_map/correct/pallas_call | solution.py:111
  84.7 0.0 all-gather.2.cloned.1.call-done.matrix_ref
  84.7 0.0 copy-start
  84.7 2.2 copy-done
  86.9 7.3 %sketch.1.sketch_ref = f32[256,128]{1,0:T(8,128)S(1)} custom-call(bf16[128,256,128]{2,1,0:T(8,128)(2,1)} %correct.1.column_ref, bf16[16384,128]{1,0:T(8,128)(2,1)S(1)} %copy-done), custom_call_target="tpu_custom_call" | custom-call | tf_op jit(solution)/shard_map/sketch/pallas_call | solution.py:174
  94.2 1.0 fusion.27
  95.2 0.0 all-reduce.4.cloned.1.call-update
  95.2 0.2 reduce-scatter.2.cloned.1.call-start
  95.5 14.3 %project.1 = f32[16384,128]{1,0:T(8,128)} custom-call(bf16[128,256,128]{2,1,0:T(8,128)(2,1)} %correct.1.column_ref, f32[256,128]{1,0:T(8,128)S(1)} %sketch.1.sketch_ref), custom_call_target="tpu_custom_call" | custom-call | tf_op jit(solution)/shard_map/project/pallas_call | solution.py:209
  109.7 0.0 reduce-scatter.2.cloned.1.call-update
  109.8 72.8 %all-reduce.4.cloned.1.call-done = f32[128,128]{0,1:T(8,128)} async-done(((f32[128,128]{0,1:T(8,128)}), f32[128,128]{0,1:T(8,128)}) %all-reduce.4.cloned.1.call-update) | async-done | bytes 65552 | tf_op jit(solution)/shard_map/psum | solution.py:228
  182.6 0.9 copy.13
  183.5 0.9 fusion.17
  184.4 11.7 %cholesky.14 = f32[128,128]{1,0:T(8,128)S(1)} custom-call(f32[128,128]{1,0:T(8,128)S(1)} %fusion.17), custom_call_target="Cholesky" | custom-call | tf_op jit(solution)/shard_map/jit(cholesky)/cholesky | solution.py:230
  196.1 0.6 compare_reduce_fusion
  196.7 0.7 fusion.11
  197.4 9.8 %custom-call.6 = f32[1,128,128]{1,2,0:T(8,128)S(1)} custom-call(f32[1,128,128]{2,1,0:T(8,128)S(1)} %fusion.11), custom_call_target="InvertDiagBlocksLowerTriangular" | custom-call | tf_op jit(solution)/shard_map/triangular_solve | solution.py:232
  207.2 0.2 fusion.15
  207.4 0.9 convolution_convert_fusion
  208.3 85.3 %reduce-scatter.2.cloned.1.call-done = f32[1024,128]{1,0:T(8,128)} async-done(((f32[16384,128]{1,0:T(8,128)}), f32[1024,128]{1,0:T(8,128)}) %reduce-scatter.2.cloned.1.call-update) | async-done | bytes 524304 | tf_op jit(solution)/shard_map/reduce_scatter | solution.py:229
  293.6 2.4 fusion.28
  (5 shorter events, 0.1 us)
Async XLA Ops:
  7.2 77.5 %all-gather.2.cloned.1.call-start = ((), (), s32[]{:S(2)}) async-start(), calls=%async_computation.1 | async-start | bytes 4456448 | tf_op jit(solution)/shard_map/all_gather | solution.py:225
  7.9 174.7 %all-reduce.4.cloned.1.call-start = ((), (), s32[]{:S(2)}) async-start(), calls=%async_computation.2 | async-start | bytes 131072 | tf_op jit(solution)/shard_map/psum | solution.py:228
  10.0 16.9 %copy-start.1 = (s32[256]{0:T(256)S(1)}, s32[256]{0:T(256)}, u32[]{:S(2)}) copy-start(s32[256]{0:T(256)} %group_ref.1) | copy-start | bytes 3076
  84.7 2.2 copy-start
  95.2 198.4 %reduce-scatter.2.cloned.1.call-start = ((), (), s32[]{:S(2)}) async-start(), calls=%async_computation.3 | async-start | bytes 8912896 | tf_op jit(solution)/shard_map/reduce_scatter | solution.py:229
Sparse Core Ops, SparseCore 0:
  10.2 53.3 all-gather.1
  95.4 87.1 all-reduce.3
  187.2 106.3 reduce-scatter.1

commit v2 on v1

v2 whole, which is shorter than its diff:
```python
import functools
import math

import jax
import jax.numpy as jnp
from jax import lax
from jax.experimental import pallas as pl
from jax.experimental.pallas import tpu as pltpu
from jax.sharding import PartitionSpec as P

AMPLITUDE = 0.1
WIENER = 0.1
F32 = jnp.float32
BF16 = jnp.bfloat16
HIGHEST = lax.Precision.HIGHEST


def real_tables(length):
    rows = jnp.arange(length, dtype=jnp.int32)
    product = rows[:, None] * rows[None, :] % length
    angles = 2.0 * math.pi / length * product.astype(F32)
    packed = jnp.where(rows[None, :] <= length // 2, jnp.cos(angles), jnp.sin(angles))
    return packed.astype(BF16)


def filter_table(defocus_values, length):
    index = jnp.arange(length, dtype=jnp.int32)
    freq = jnp.where(index < length // 2, index, index - length).astype(F32) / length
    phase = jnp.pi * defocus_values[:, None] * (freq * freq)[None, :]
    sine, cosine = lax.optimization_barrier((jnp.sin(phase), jnp.cos(phase)))
    keep = math.sqrt(1.0 - AMPLITUDE**2)
    first = (keep * sine + AMPLITUDE * cosine)[:, :, None]
    second = (keep * cosine - AMPLITUDE * sine)[:, :, None]
    contrast = -(first * cosine[:, None, :] + second * sine[:, None, :])
    wiener = (contrast / (contrast * contrast + WIENER)).astype(BF16).astype(F32)
    twice = jnp.where((index == 0) | (index == length // 2), 1.0, 2.0).astype(F32)
    return (wiener * (twice[:, None] * twice[None, :] / float(length * length))).astype(BF16)


def correct_kernel(
    group_ref,
    live_ref,
    image_ref,
    filters,
    pair_ref,
    pair_t_ref,
    table_ref,
    table_t_ref,
    out_ref,
    turned,
):
    step = pl.program_id(0)
    count, length, _ = image_ref.shape
    pairs = count // 2
    base = step * count

    def side_by_side(parts):
        return jnp.concatenate(parts, axis=1)

    def stacked(wide):
        return jnp.concatenate(
            [wide[:, 2 * length * i : 2 * length * (i + 1)] for i in range(pairs)], axis=0
        )

    def unstacked(tall):
        return side_by_side([tall[length * i : length * (i + 1)] for i in range(pairs)])

    images = jnp.concatenate(
        [side_by_side([image_ref[2 * i], image_ref[2 * i + 1]]) for i in range(pairs)], axis=0
    )
    rows = jnp.dot(images, pair_ref[...], preferred_element_type=F32).astype(BF16)
    spectrum = jnp.dot(table_t_ref[...], unstacked(rows), preferred_element_type=F32)
    weights = side_by_side([filters[group_ref[base + i]] for i in range(count)])
    kept = (spectrum * weights.astype(F32)).astype(BF16)
    back = jnp.dot(stacked(kept), pair_t_ref[...], preferred_element_type=F32).astype(BF16)
    result = jnp.dot(table_ref[...], unstacked(back), preferred_element_type=F32)
    for i in range(count):
        turned[pl.ds(i, length, stride=count), :] = result[:, i * length : (i + 1) * length]
    slot = base + lax.broadcasted_iota(jnp.int32, (1, count, 1), 1)
    values = turned[...].reshape(length, count, length)
    out_ref[...] = jnp.where(slot < live_ref[0], values, 0.0).astype(BF16)


def correct(images, groups, live, defocus_values):
    slots, length, _ = images.shape
    count = math.gcd(slots, 16)
    table = real_tables(length)
    zero = jnp.zeros_like(table)
    pair = jnp.concatenate(
        [jnp.concatenate([table, zero], axis=1), jnp.concatenate([zero, table], axis=1)], axis=0
    )
    number = defocus_values.shape[0]

    def whole(*shape):
        return pl.BlockSpec(shape, lambda i, *_: (0,) * len(shape))

    return pl.pallas_call(
        correct_kernel,
        out_shape=jax.ShapeDtypeStruct((length, slots, length), BF16),
        grid_spec=pltpu.PrefetchScalarGridSpec(
            num_scalar_prefetch=2,
            grid=(slots // count,),
            in_specs=[
                pl.BlockSpec((count, length, length), lambda i, *_: (i, 0, 0)),
                whole(number, length, length),
                whole(2 * length, 2 * length),
                whole(2 * length, 2 * length),
                whole(length, length),
                whole(length, length),
            ],
            out_specs=pl.BlockSpec((length, count, length), lambda i, *_: (0, i, 0)),
            scratch_shapes=[pltpu.VMEM((length * count, length), F32)],
        ),
        compiler_params=pltpu.CompilerParams(vmem_limit_bytes=48 << 20),
        cost_estimate=pl.CostEstimate(
            flops=16 * slots * length**3, bytes_accessed=4 * slots * length**2, transcendentals=0
        ),
        name="correct",
    )(groups, live, images, filter_table(defocus_values, length), pair, pair.T, table, table.T)


def sketch_kernel(column_ref, matrix_ref, sketch_ref):
    @pl.when(pl.program_id(0) == 0)
    def _():
        sketch_ref[...] = jnp.zeros_like(sketch_ref)

    count, _, length = column_ref.shape
    total = sketch_ref[...]
    for pair in range(count // 2):
        left = jnp.concatenate([column_ref[2 * pair], column_ref[2 * pair + 1]], axis=1)
        right = matrix_ref[pl.ds(2 * pair * length, 2 * length), :]
        total += jnp.dot(left, right, preferred_element_type=F32)
    sketch_ref[...] = total


def make_sketch(columns, matrix):
    length, slots, _ = columns.shape
    rank = matrix.shape[1]
    count = math.gcd(length, 16)
    return pl.pallas_call(
        sketch_kernel,
        out_shape=jax.ShapeDtypeStruct((slots, rank), F32),
        grid=(length // count,),
        in_specs=[
            pl.BlockSpec((count, slots, length), lambda i: (i, 0, 0)),
            pl.BlockSpec((count * length, rank), lambda i: (i, 0)),
        ],
        out_specs=pl.BlockSpec((slots, rank), lambda i: (0, 0)),
        compiler_params=pltpu.CompilerParams(vmem_limit_bytes=48 << 20),
        name="sketch",
    )(columns, matrix)


def bits_of(size):
    return size.bit_length() - 1


def partner_of(me, mask):
    for shift in range(mask.bit_length()):
        bit = 1 << shift
        if mask & bit:
            me = me + bit * (1 - 2 * lax.rem(lax.div(me, bit), 2))
    return me


def greet(me, size):
    barrier = pltpu.get_barrier_semaphore()
    for shift in range(bits_of(size)):
        pl.semaphore_signal(
            barrier,
            inc=1,
            device_id={"pix": partner_of(me, 1 << shift)},
            device_id_type=pl.DeviceIdType.MESH,
        )
    pl.semaphore_wait(barrier, bits_of(size))


def sum_kernel(size, part_ref, out_ref, arrived, send_sem, recv_sem):
    me = lax.axis_index("pix")
    greet(me, size)
    out_ref[...] = part_ref[...]
    for stage in range(bits_of(size)):
        copy = pltpu.make_async_remote_copy(
            src_ref=out_ref,
            dst_ref=arrived.at[stage],
            send_sem=send_sem.at[stage],
            recv_sem=recv_sem.at[stage],
            device_id={"pix": partner_of(me, 1 << stage)},
            device_id_type=pl.DeviceIdType.MESH,
        )
        copy.start()
        copy.wait()
        out_ref[...] += arrived[stage]


def sum_over_shards(part, size):
    stages = bits_of(size)
    return pl.pallas_call(
        functools.partial(sum_kernel, size),
        out_shape=jax.ShapeDtypeStruct(part.shape, part.dtype),
        in_specs=[pl.BlockSpec(memory_space=pltpu.VMEM)],
        out_specs=pl.BlockSpec(memory_space=pltpu.VMEM),
        scratch_shapes=[
            pltpu.VMEM((stages,) + part.shape, part.dtype),
            pltpu.SemaphoreType.DMA((stages,)),
            pltpu.SemaphoreType.DMA((stages,)),
        ],
        compiler_params=pltpu.CompilerParams(collective_id=0, has_side_effects=True),
        name="sum_over_shards",
    )(part)


def halving_orders(size):
    bits = [1 << shift for shift in range(bits_of(size))]
    if len(bits) < 3:
        return (bits, bits)
    return (bits, bits[:1] + bits[2:] + bits[1:2])


def masks_of(bits):
    if not bits:
        return [0]
    rest = masks_of(bits[1:])
    return [bits[0] | mask for mask in rest] + rest


def project_kernel(size, basis_ref, column_ref, out_ref, held, arrived, send_sem, recv_sem):
    me = lax.axis_index("pix")
    length = column_ref.shape[0]
    rows = length // size
    part = rows // 2
    orders = halving_orders(size)
    slots = {}
    for half in range(2):
        for stage in range(len(orders[half])):
            for mask in masks_of(orders[half][stage + 1 :]):
                slots[half, stage, mask] = len(slots) % (size - 1)

    def copy_of(half, stage, mask):
        bit = orders[half][stage]
        slot = slots[half, stage, mask]
        return pltpu.make_async_remote_copy(
            src_ref=held.at[half, bit | mask],
            dst_ref=arrived.at[half, slot],
            send_sem=send_sem.at[half, slot],
            recv_sem=recv_sem.at[half, slot],
            device_id={"pix": partner_of(me, bit)},
            device_id_type=pl.DeviceIdType.MESH,
        )

    greet(me, size)
    first = orders[0][0]
    order = masks_of([first] + orders[0][1:])
    for mask in order:
        start = partner_of(me, mask) * rows
        for half in range(2):
            right = jnp.concatenate(
                [column_ref[start + half * part + row] for row in range(part)], axis=1
            )
            held[half, mask] = jnp.dot(
                basis_ref[...], right, preferred_element_type=F32
            ).astype(BF16)
            if mask & first:
                copy_of(half, 0, mask - first).start()

    for stage in range(bits_of(size)):
        for half in range(2):
            later = orders[half][stage + 1 :]
            for mask in masks_of(later):
                copy_of(half, stage, mask).wait_recv()
                total = (
                    held[half, mask].astype(F32)
                    + arrived[half, slots[half, stage, mask]].astype(F32)
                )
                if later:
                    held[half, mask] = total.astype(BF16)
                    if mask & later[0]:
                        copy_of(half, stage + 1, mask - later[0]).start()
                else:
                    turned = total.T
                    height = out_ref.shape[0] // 2
                    out_ref[half * height : (half + 1) * height, :] = turned
    for half in range(2):
        for stage in range(bits_of(size)):
            for mask in masks_of(orders[half][stage + 1 :]):
                copy_of(half, stage, mask).wait_send()


def project(columns, basis, size):
    length, slots, _ = columns.shape
    rank = basis.shape[1]
    width = length * length // size
    return pl.pallas_call(
        functools.partial(project_kernel, size),
        out_shape=jax.ShapeDtypeStruct((width, rank), F32),
        in_specs=[pl.BlockSpec(memory_space=pltpu.VMEM)] * 2,
        out_specs=pl.BlockSpec(memory_space=pltpu.VMEM),
        scratch_shapes=[
            pltpu.VMEM((2, size, rank, width // 2), BF16),
            pltpu.VMEM((2, size - 1, rank, width // 2), BF16),
            pltpu.SemaphoreType.DMA((2, size - 1)),
            pltpu.SemaphoreType.DMA((2, size - 1)),
        ],
        compiler_params=pltpu.CompilerParams(
            collective_id=1, has_side_effects=True, vmem_limit_bytes=48 << 20
        ),
        name="project",
    )(basis.T, columns)


def per_device(particle_images, defocus_group, live_counts, defocus_values, test_matrix):
    size = lax.axis_size("pix")
    matrix = lax.all_gather(test_matrix, "pix", axis=0, tiled=True)
    columns = correct(particle_images, defocus_group, live_counts, defocus_values)
    sketch = make_sketch(columns, matrix)
    gram = sum_over_shards(jnp.dot(sketch.T, sketch, precision=HIGHEST), size)
    factor_low = jnp.linalg.cholesky(gram)
    rank = gram.shape[0]
    inverse_t = lax.linalg.triangular_solve(
        factor_low, jnp.eye(rank, dtype=F32), left_side=False, lower=True, transpose_a=True
    )
    range_basis = jnp.dot(sketch, inverse_t, precision=HIGHEST).astype(BF16)
    return (range_basis, project(columns, range_basis, size))


def solution(mesh):
    placed = (
        P(("grp", "pix"), None, None),
        P(("grp", "pix")),
        P(("grp", "pix")),
        P("grp"),
        P(("grp", "pix"), None),
    )
    return jax.shard_map(
        per_device,
        mesh=mesh,
        in_specs=placed,
        out_specs=(P(("grp", "pix"), None), P(("grp", "pix"), None)),
        check_vma=False,
    )
```

time: 303 us -> 166 us (0.55)
  waiting for transfers between devices: 159 us -> 29 us
  other arithmetic: 41.9 us -> 27.5 us
  Pallas kernels: 79.3 us -> 86.3 us
    reduce_scatter x1 -> x0, waiting for transfers between devices: 85.3 us -> none  [per_device(): lax.psum_scatter(project(columns, sketch), 'pix', scatter_dimension=0, ti...]
    psum x1 -> x0, waiting for transfers between devices: 72.8 us -> none  [per_device(): gram = lax.psum(jnp.dot(sketch.T, sketch, precision=HIGHEST), 'pix')]
    pallas_call x1 -> x2, Pallas kernels: 14.3 us -> 57 us  [the longest x1 41.7 us: project(): pl.pallas_call(functools.partial(project_kernel, size), out_shape=jax.Sha...]
    pallas_call x1, Pallas kernels: 57.8 us -> 21.9 us  [correct(): pl.pallas_call(correct_kernel, out_shape=jax.ShapeDtypeStruct((length, sl...]
    all_gather x1, waiting for transfers between devices: 0.01 us -> 28.4 us  [per_device(): matrix = lax.all_gather(test_matrix, 'pix', axis=0, tiled=True)]
    neg x1 -> x0, other arithmetic: 16.9 us -> none  [phase_tables(): second = -(keep * cosine - AMPLITUDE * sine)]
  transfers between devices with their start and end apart: 3 -> 1, of which waited for: 2 -> 1; matrix products, arithmetic and copies ran while one was open for 15% -> 2% of each run, Pallas kernels for 24% -> 13%
where the time goes in v2:
time: 166 us; the launch traced here: 165 us
  Pallas kernels  86.3 us (52%)
  waiting for transfers between devices  29 us (17%)
  other arithmetic  27.5 us (17%)
  between operations  14.8 us (9%)
  local copies, waits for them, and re-layouts  5.42 us (3%)
    pallas_call x1, Pallas kernels, project(): pl.pallas_call(functools.partial(project_kernel, size), out_shape=jax.Sha...  41.7 us
    all_gather x1, waiting for transfers between devices, per_device(): matrix = lax.all_gather(test_matrix, 'pix', axis=0, tiled=True)  28.4 us
    pallas_call x1, Pallas kernels, correct(): pl.pallas_call(correct_kernel, out_shape=jax.ShapeDtypeStruct((length, sl...  21.9 us
    pallas_call x1, Pallas kernels, sum_over_shards(): pl.pallas_call(functools.partial(sum_kernel, size), out_shape=jax.ShapeDt...  15.2 us
    another operation x3, other arithmetic, per_device(): factor_low = jnp.linalg.cholesky(gram)  12.4 us
    another operation x2, other arithmetic, per_device(): lax.linalg.triangular_solve(factor_low, jnp.eye(rank, dtype=F32), left_si...  10.5 us
    pallas_call x1, Pallas kernels, make_sketch(): pl.pallas_call(sketch_kernel, out_shape=jax.ShapeDtypeStruct((slots, rank...  7.48 us
    unnamed x6, local copies, waits for them, and re-layouts  4.39 us
  transfers between devices with their start and end apart: 1, of which 1 were waited for; matrix products, arithmetic and copies ran while one was open for 2% of the time, Pallas kernels for 13%

profile of v2, /device:TPU:0, one launch (start us, length us, event | category | flops | bytes accessed | tf_op | source)
XLA Modules:
  0.0 164.7 jit_solution(7286964240212041924)
XLA Ops:
  7.2 0.0 all-gather.2.cloned.1.call-start
  7.2 0.7 all-gather.2.cloned.1.call-update
  7.9 0.7 broadcast_multiply_fusion
  8.6 0.2 multiply_cosine_fusion
  8.8 0.3 select_convert_fusion
  9.1 0.1 copy.7.pair_t_ref
  9.9 0.1 multiply_multiply_fusion
  10.0 2.5 %multiply_convert_fusion.filters = bf16[64,128,128]{2,1,0:T(8,128)(2,1)S(1)} fusion(f32[128,128]{1,0:T(8,128)S(1)} %multiply_multiply_fusion, f32[64,128]{1,0:T(8,128)S(1)} %get-tuple-element.4, f32[64,128]{1,0:T(8,128)S(1)} %get-tuple-element.9, f32[64,128]{1,0:T(8,128)S(1)} %get-tuple-element.5, f32[64,128]{1,0:T(8,128)S(1)} %get-tuple-element.8), kind=kLoop, calls=%fused_computation | loop fusion | flops 11534336 | bytes 2293760 | tf_op jit(solution)/shard_map/convert_element_type | solution.py:37
  12.5 0.0 copy-start.1
  12.5 0.7 copy-done.1
  13.2 21.9 %correct.1.column_ref = bf16[128,256,128]{2,1,0:T(8,128)(2,1)} custom-call(s32[256]{0:T(256)S(1)} %copy-done.1, s32[1]{0:T(128)S(6)} %copy.13.live_ref, bf16[256,128,128]{2,1,0:T(8,128)(2,1)} %image_ref.1, bf16[64,128,128]{2,1,0:T(8,128)(2,1)S(1)} %multiply_convert_fusion.filters, bf16[256,256]{1,0:T(8,128)(2,1)S(1)} %get-tuple-element.11.pair_ref, ...), custom_call_target="tpu_custom_call" | custom-call | flops 8589934592 | bytes 16777216 | tf_op jit(solution)/shard_map/correct/pallas_call | solution.py:97
  35.1 28.4 %all-gather.2.cloned.1.call-done.matrix_ref = bf16[16384,128]{1,0:T(8,128)(2,1)} async-done(((bf16[1024,128]{1,0:T(8,128)(2,1)}), bf16[16384,128]{1,0:T(8,128)(2,1)}) %all-gather.2.cloned.1.call-update) | async-done | bytes 4194320 | tf_op jit(solution)/shard_map/all_gather | solution.py:313
  63.5 0.0 copy-start
  63.5 2.2 %copy-done = bf16[16384,128]{1,0:T(8,128)(2,1)S(1)} copy-done((bf16[16384,128]{1,0:T(8,128)(2,1)S(1)}, bf16[16384,128]{1,0:T(8,128)(2,1)}, u32[]{:S(2)}) %copy-start) | copy-done | bytes 4194328
  65.6 7.5 %sketch.1 = f32[256,128]{1,0:T(8,128)S(1)} custom-call(bf16[128,256,128]{2,1,0:T(8,128)(2,1)} %correct.1.column_ref, bf16[16384,128]{1,0:T(8,128)(2,1)S(1)} %copy-done), custom_call_target="tpu_custom_call" | custom-call | tf_op jit(solution)/shard_map/sketch/pallas_call | solution.py:140
  73.1 1.0 fusion.19.part_ref
  74.1 15.2 %sum_over_shards.1 = f32[128,128]{1,0:T(8,128)} custom-call(f32[128,128]{1,0:T(8,128)} %fusion.19.part_ref), custom_call_target="tpu_custom_call" | custom-call | tf_op jit(solution)/shard_map/sum_over_shards/pallas_call | solution.py:198
  89.4 0.9 copy.8
  90.3 0.9 fusion.9
  91.2 11.7 %cholesky.14 = f32[128,128]{1,0:T(8,128)S(1)} custom-call(f32[128,128]{1,0:T(8,128)S(1)} %fusion.9), custom_call_target="Cholesky" | custom-call | tf_op jit(solution)/shard_map/jit(cholesky)/cholesky | solution.py:317
  102.9 0.6 compare_reduce_fusion
  103.6 0.7 fusion.3
  104.2 9.8 %custom-call.6 = f32[1,128,128]{1,2,0:T(8,128)S(1)} custom-call(f32[1,128,128]{2,1,0:T(8,128)S(1)} %fusion.3), custom_call_target="InvertDiagBlocksLowerTriangular" | custom-call | tf_op jit(solution)/shard_map/triangular_solve | solution.py:319
  114.0 0.2 fusion.7
  114.2 0.3 convolution_convert_fusion
  114.6 0.7 copy.10
  115.3 41.7 %project.1 = f32[1024,128]{1,0:T(8,128)S(1)} custom-call(bf16[128,256]{1,0:T(8,128)(2,1)S(1)} %bitcast.16, bf16[128,256,128]{2,1,0:T(8,128)(2,1)} %correct.1.column_ref), custom_call_target="tpu_custom_call" | custom-call | tf_op jit(solution)/shard_map/project/pallas_call | solution.py:293
  157.0 0.8 copy.14
  (6 shorter events, 0.1 us)
Async XLA Ops:
  7.2 56.3 %all-gather.2.cloned.1.call-start = ((), (), s32[]{:S(2)}) async-start(), calls=%async_computation | async-start | bytes 4456448 | tf_op jit(solution)/shard_map/all_gather | solution.py:313
  12.5 0.7 copy-start.1
  63.5 2.2 %copy-start = (bf16[16384,128]{1,0:T(8,128)(2,1)S(1)}, bf16[16384,128]{1,0:T(8,128)(2,1)}, u32[]{:S(2)}) copy-start(bf16[16384,128]{1,0:T(8,128)(2,1)} %all-gather.2.cloned.1.call-done.matrix_ref) | copy-start | bytes 12582916
Sparse Core Ops, SparseCore 0:
  10.2 53.2 all-gather.1

commit v3 on v2

--- a/solution.py
+++ b/solution.py
@@ -37,25 +37,200 @@
     return (wiener * (twice[:, None] * twice[None, :] / float(length * length))).astype(BF16)
 
 
-def correct_kernel(
+def bits_of(size):
+    return size.bit_length() - 1
+
+
+def partner_of(me, mask):
+    for shift in range(mask.bit_length()):
+        bit = 1 << shift
+        if mask & bit:
+            me = me + bit * (1 - 2 * lax.rem(lax.div(me, bit), 2))
+    return me
+
+
+def greet(me, masks):
+    barrier = pltpu.get_barrier_semaphore()
+    for mask in masks:
+        pl.semaphore_signal(
+            barrier,
+            inc=1,
+            device_id={"pix": partner_of(me, mask)},
+            device_id_type=pl.DeviceIdType.MESH,
+        )
+    pl.semaphore_wait(barrier, len(masks))
+
+
+def remote(src, dst, send_sem, recv_sem, peer):
+    return pltpu.make_async_remote_copy(
+        src_ref=src,
+        dst_ref=dst,
+        send_sem=send_sem,
+        recv_sem=recv_sem,
+        device_id={"pix": peer},
+        device_id_type=pl.DeviceIdType.MESH,
+    )
+
+
+def halving_orders(size):
+    bits = [1 << shift for shift in range(bits_of(size))]
+    if len(bits) < 3:
+        return (bits, bits)
+    return (bits, bits[:1] + bits[2:] + bits[1:2])
+
+
+def masks_of(bits):
+    if not bits:
+        return [0]
+    rest = masks_of(bits[1:])
+    return [bits[0] | mask for mask in rest] + rest
+
+
+def gathering_orders(size):
+    first, second = halving_orders(size)
+    return (first[::-1], second[1:][::-1] + second[:1])
+
+
+def sums(bits):
+    out = [0]
+    for bit in bits:
+        out = out + [bit | mask for mask in out]
+    return out
+
+
+def direct_sum(rank, size):
+    return rank % (8 * size) == 0
+
+
+def peers(rank, size):
+    if direct_sum(rank, size):
+        return list(range(1, size))
+    return [1 << shift for shift in range(bits_of(size))]
+
+
+def sum_gram(me, size, gram_ref, parts, arrived, send_sem, recv_sem):
+    if not direct_sum(parts.shape[0] * parts.shape[1], size):
+        gram_ref[...] = parts[...].reshape(gram_ref.shape)
+        for stage in range(bits_of(size)):
+            copy = remote(
+                gram_ref,
+                arrived.at[stage],
+                send_sem.at[stage],
+                recv_sem.at[stage],
+                partner_of(me, 1 << stage),
+            )
+            copy.start()
+            copy.wait()
+            gram_ref[...] += arrived[stage]
+        return
+    height = parts.shape[1]
+    scatter = [
+        remote(
+            parts.at[partner_of(me, d)],
+            arrived.at[d],
+            send_sem.at[d],
+            recv_sem.at[d],
+            partner_of(me, d),
+        )
+        for d in range(1, size)
+    ]
+    for copy in scatter:
+        copy.start()
+    total = parts[me]
+    for d, copy in enumerate(scatter, 1):
+        copy.wait_recv()
+        total = total + arrived[d]
+    arrived[0] = total
+    own = pl.ds(pl.multiple_of(me * height, height), height)
+    gather = [
+        remote(
+            arrived.at[0],
+            gram_ref.at[own],
+            send_sem.at[size + d],
+            recv_sem.at[size + d],
+            partner_of(me, d),
+        )
+        for d in range(1, size)
+    ]
+    for copy in gather:
+        copy.start()
+    gram_ref[own, :] = total
+    for copy in gather:
+        copy.wait_recv()
+    for copy in scatter + gather:
+        copy.wait_send()
+
+
+def sketch_kernel(
+    size,
     group_ref,
     live_ref,
     image_ref,
+    matrix_ref,
     filters,
     pair_ref,
     pair_t_ref,
     table_ref,
     table_t_ref,
     out_ref,
+    sketch_ref,
+    gram_ref,
     turned,
+    held,
+    summed,
+    parts,
+    arrived,
+    send_sem,
+    recv_sem,
+    sum_send_sem,
+    sum_recv_sem,
 ):
+    me = lax.axis_index("pix")
     step = pl.program_id(0)
+    steps = out_ref.shape[1] // image_ref.shape[0]
     count, length, _ = image_ref.shape
     pairs = count // 2
     base = step * count
-
-    def side_by_side(parts):
-        return jnp.concatenate(parts, axis=1)
+    orders = gathering_orders(size)
+    stages = bits_of(size)
+    height = matrix_ref.shape[0] // 2
+
+    def copy_of(half, stage, mask):
+        bit = orders[half][stage]
+        slot = (bit | mask) - 1
+        return remote(
+            held.at[half, mask],
+            held.at[half, bit | mask],
+            send_sem.at[half, slot],
+            recv_sem.at[half, slot],
+            partner_of(me, bit),
+        )
+
+    def receive(stage, half, mask):
+        copy_of(half, stage, mask).wait_recv()
+        for later in range(stage + 1, stages):
+            copy_of(half, later, orders[half][stage] | mask).start()
+
+    @pl.when(step == 0)
+    def _():
+        greet(me, peers(gram_ref.shape[0], size))
+        for half in range(2):
+            held[half, 0] = matrix_ref[half * height : (half + 1) * height, :]
+        for stage in range(stages):
+            for half in range(2):
+                copy_of(half, stage, 0).start()
+
+    early = min(2, stages)
+    for stage in range(early):
+
+        @pl.when(step == steps * (5 + 6 * stage) // 16)
+        def _(stage=stage):
+            for place in range(1 << stage):
+                for half in range(2):
+                    receive(stage, half, sums(orders[half][:stage])[place])
+
+    def side_by_side(values):
+        return jnp.concatenate(values, axis=1)
 
     def stacked(wide):
         return jnp.concatenate(
@@ -78,11 +253,46 @@
         turned[pl.ds(i, length, stride=count), :] = result[:, i * length : (i + 1) * length]
     slot = base + lax.broadcasted_iota(jnp.int32, (1, count, 1), 1)
     values = turned[...].reshape(length, count, length)
-    out_ref[...] = jnp.where(slot < live_ref[0], values, 0.0).astype(BF16)
-
-
-def correct(images, groups, live, defocus_values):
+    out_ref[:, pl.ds(pl.multiple_of(base, count), count), :] = jnp.where(
+        slot < live_ref[0], values, 0.0
+    ).astype(BF16)
+
+    @pl.when(step == steps - 1)
+    def _():
+        lines = length // size
+        part = lines // 2
+
+        def term(half, mask):
+            start = partner_of(me, mask) * lines + half * part
+            left = side_by_side([out_ref[start + line] for line in range(part)])
+            return jnp.dot(left, held[half, mask], preferred_element_type=F32)
+
+        sketch_ref[...] = jnp.zeros_like(sketch_ref)
+        for half in range(2):
+            for mask in sums(orders[half][:early]):
+                sketch_ref[...] += term(half, mask)
+        for stage in range(early, stages):
+            for place in range(1 << stage):
+                for half in range(2):
+                    mask = sums(orders[half][:stage])[place]
+                    receive(stage, half, mask)
+                    sketch_ref[...] += term(half, orders[half][stage] | mask)
+        sketch = sketch_ref[...]
+        gram = lax.dot_general(
+            sketch, sketch, (((0,), (0,)), ((), ())), precision=HIGHEST, preferred_element_type=F32
+        )
+        parts[...] = gram.reshape(parts.shape)
+        sum_gram(me, size, summed, parts, arrived, sum_send_sem, sum_recv_sem)
+        gram_ref[...] = summed[...]
+        for half in range(2):
+            for stage in range(stages):
+                for mask in sums(orders[half][:stage]):
+                    copy_of(half, stage, mask).wait_send()
+
+
+def make_sketch(images, groups, live, defocus_values, matrix, size):
     slots, length, _ = images.shape
+    height, rank = matrix.shape
     count = math.gcd(slots, 16)
     table = real_tables(length)
     zero = jnp.zeros_like(table)
@@ -90,138 +300,68 @@
         [jnp.concatenate([table, zero], axis=1), jnp.concatenate([zero, table], axis=1)], axis=0
     )
     number = defocus_values.shape[0]
+    if direct_sum(rank, size):
+        summing = [
+            pltpu.VMEM((size, rank // size, rank), F32),
+            pltpu.VMEM((size, rank // size, rank), F32),
+        ]
+        signals = 2 * size
+    else:
+        summing = [
+            pltpu.VMEM((1, rank, rank), F32),
+            pltpu.VMEM((bits_of(size), rank, rank), F32),
+        ]
+        signals = bits_of(size)
 
     def whole(*shape):
         return pl.BlockSpec(shape, lambda i, *_: (0,) * len(shape))
 
     return pl.pallas_call(
-        correct_kernel,
-        out_shape=jax.ShapeDtypeStruct((length, slots, length), BF16),
+        functools.partial(sketch_kernel, size),
+        out_shape=(
+            jax.ShapeDtypeStruct((length, slots, length), BF16),
+            jax.ShapeDtypeStruct((slots, rank), F32),
+            jax.ShapeDtypeStruct((rank, rank), F32),
+        ),
         grid_spec=pltpu.PrefetchScalarGridSpec(
             num_scalar_prefetch=2,
             grid=(slots // count,),
             in_specs=[
                 pl.BlockSpec((count, length, length), lambda i, *_: (i, 0, 0)),
+                whole(height, rank),
                 whole(number, length, length),
                 whole(2 * length, 2 * length),
                 whole(2 * length, 2 * length),
                 whole(length, length),
                 whole(length, length),
             ],
-            out_specs=pl.BlockSpec((length, count, length), lambda i, *_: (0, i, 0)),
-            scratch_shapes=[pltpu.VMEM((length * count, length), F32)],
+            out_specs=(whole(length, slots, length), whole(slots, rank), whole(rank, rank)),
+            scratch_shapes=[
+                pltpu.VMEM((length * count, length), F32),
+                pltpu.VMEM((2, size, height // 2, rank), BF16),
+                pltpu.VMEM((rank, rank), F32),
+                *summing,
+                pltpu.SemaphoreType.DMA((2, size - 1)),
+                pltpu.SemaphoreType.DMA((2, size - 1)),
+                pltpu.SemaphoreType.DMA((signals,)),
+                pltpu.SemaphoreType.DMA((signals,)),
+            ],
         ),
-        compiler_params=pltpu.CompilerParams(vmem_limit_bytes=48 << 20),
-        cost_estimate=pl.CostEstimate(
-            flops=16 * slots * length**3, bytes_accessed=4 * slots * length**2, transcendentals=0
+        compiler_params=pltpu.CompilerParams(
+            collective_id=0, has_side_effects=True, vmem_limit_bytes=50 << 20
         ),
-        name="correct",
-    )(groups, live, images, filter_table(defocus_values, length), pair, pair.T, table, table.T)
-
-
-def sketch_kernel(column_ref, matrix_ref, sketch_ref):
-    @pl.when(pl.program_id(0) == 0)
-    def _():
-        sketch_ref[...] = jnp.zeros_like(sketch_ref)
-
-    count, _, length = column_ref.shape
-    total = sketch_ref[...]
-    for pair in range(count // 2):
-        left = jnp.concatenate([column_ref[2 * pair], column_ref[2 * pair + 1]], axis=1)
-        right = matrix_ref[pl.ds(2 * pair * length, 2 * length), :]
-        total += jnp.dot(left, right, preferred_element_type=F32)
-    sketch_ref[...] = total
-
-
-def make_sketch(columns, matrix):
-    length, slots, _ = columns.shape
-    rank = matrix.shape[1]
-    count = math.gcd(length, 16)
-    return pl.pallas_call(
-        sketch_kernel,
-        out_shape=jax.ShapeDtypeStruct((slots, rank), F32),
-        grid=(length // count,),
-        in_specs=[
-            pl.BlockSpec((count, slots, length), lambda i: (i, 0, 0)),
-            pl.BlockSpec((count * length, rank), lambda i: (i, 0)),
-        ],
-        out_specs=pl.BlockSpec((slots, rank), lambda i: (0, 0)),
-        compiler_params=pltpu.CompilerParams(vmem_limit_bytes=48 << 20),
         name="sketch",
-    )(columns, matrix)
-
-
-def bits_of(size):
-    return size.bit_length() - 1
-
-
-def partner_of(me, mask):
-    for shift in range(mask.bit_length()):
-        bit = 1 << shift
-        if mask & bit:
-            me = me + bit * (1 - 2 * lax.rem(lax.div(me, bit), 2))
-    return me
-
-
-def greet(me, size):
-    barrier = pltpu.get_barrier_semaphore()
-    for shift in range(bits_of(size)):
-        pl.semaphore_signal(
-            barrier,
-            inc=1,
-            device_id={"pix": partner_of(me, 1 << shift)},
-            device_id_type=pl.DeviceIdType.MESH,
-        )
-    pl.semaphore_wait(barrier, bits_of(size))
-
-
-def sum_kernel(size, part_ref, out_ref, arrived, send_sem, recv_sem):
-    me = lax.axis_index("pix")
-    greet(me, size)
-    out_ref[...] = part_ref[...]
-    for stage in range(bits_of(size)):
-        copy = pltpu.make_async_remote_copy(
-            src_ref=out_ref,
-            dst_ref=arrived.at[stage],
-            send_sem=send_sem.at[stage],
-            recv_sem=recv_sem.at[stage],
-            device_id={"pix": partner_of(me, 1 << stage)},
-            device_id_type=pl.DeviceIdType.MESH,
-        )
-        copy.start()
-        copy.wait()
-        out_ref[...] += arrived[stage]
-
-
-def sum_over_shards(part, size):
-    stages = bits_of(size)
-    return pl.pallas_call(
-        functools.partial(sum_kernel, size),
-        out_shape=jax.ShapeDtypeStruct(part.shape, part.dtype),
-        in_specs=[pl.BlockSpec(memory_space=pltpu.VMEM)],
-        out_specs=pl.BlockSpec(memory_space=pltpu.VMEM),
-        scratch_shapes=[
-            pltpu.VMEM((stages,) + part.shape, part.dtype),
-            pltpu.SemaphoreType.DMA((stages,)),
-            pltpu.SemaphoreType.DMA((stages,)),
-        ],
-        compiler_params=pltpu.CompilerParams(collective_id=0, has_side_effects=True),
-        name="sum_over_shards",
-    )(part)
-
-
-def halving_orders(size):
-    bits = [1 << shift for shift in range(bits_of(size))]
-    if len(bits) < 3:
-        return (bits, bits)
-    return (bits, bits[:1] + bits[2:] + bits[1:2])
-
-
-def masks_of(bits):
-    if not bits:
-        return [0]
-    rest = masks_of(bits[1:])
-    return [bits[0] | mask for mask in rest] + rest
+    )(
+        groups,
+        live,
+        images,
+        matrix,
+        filter_table(defocus_values, length),
+        pair,
+        pair.T,
+        table,
+        table.T,
+    )
 
 
 def project_kernel(size, basis_ref, column_ref, out_ref, held, arrived, send_sem, recv_sem):
@@ -239,16 +379,15 @@
     def copy_of(half, stage, mask):
         bit = orders[half][stage]
         slot = slots[half, stage, mask]
-        return pltpu.make_async_remote_copy(
-            src_ref=held.at[half, bit | mask],
-            dst_ref=arrived.at[half, slot],
-            send_sem=send_sem.at[half, slot],
-            recv_sem=recv_sem.at[half, slot],
-            device_id={"pix": partner_of(me, bit)},
-            device_id_type=pl.DeviceIdType.MESH,
-        )
-
-    greet(me, size)
+        return remote(
+            held.at[half, bit | mask],
+            arrived.at[half, slot],
+            send_sem.at[half, slot],
+            recv_sem.at[half, slot],
+            partner_of(me, bit),
+        )
+
+    greet(me, [1 << shift for shift in range(bits_of(size))])
     first = orders[0][0]
     order = masks_of([first] + orders[0][1:])
     for mask in order:
@@ -310,10 +449,9 @@
 
 def per_device(particle_images, defocus_group, live_counts, defocus_values, test_matrix):
     size = lax.axis_size("pix")
-    matrix = lax.all_gather(test_matrix, "pix", axis=0, tiled=True)
-    columns = correct(particle_images, defocus_group, live_counts, defocus_values)
-    sketch = make_sketch(columns, matrix)
-    gram = sum_over_shards(jnp.dot(sketch.T, sketch, precision=HIGHEST), size)
+    columns, sketch, gram = make_sketch(
+        particle_images, defocus_group, live_counts, defocus_values, test_matrix, size
+    )
     factor_low = jnp.linalg.cholesky(gram)
     rank = gram.shape[0]
     inverse_t = lax.linalg.triangular_solve(

time: 166 us -> 125 us (0.75)
  waiting for transfers between devices: 29 us -> 0 us
  between operations: 14.8 us -> 1.41 us
  Pallas kernels: 86.3 us -> 92.8 us
  local copies, waits for them, and re-layouts: 5.42 us -> 3.34 us
    all_gather x1 -> x0, waiting for transfers between devices: 28.4 us -> none  [per_device(): matrix = lax.all_gather(test_matrix, 'pix', axis=0, tiled=True)]
    pallas_call x3 -> x1, Pallas kernels: 44.6 us -> 52.2 us  [make_sketch(): pl.pallas_call(functools.partial(sketch_kernel, size), out_shape=(jax.Sha...]
  transfers between devices with their start and end apart: 1 -> 0, of which waited for: 1 -> 0; matrix products, arithmetic and copies ran while one was open for 2% -> 0% of each run, Pallas kernels for 13% -> 0%
where the time goes in v3:
time: 125 us
  Pallas kernels  92.8 us (74%)
  other arithmetic  26.6 us (21%)
  local copies, waits for them, and re-layouts  3.34 us (3%)
  between operations  1.41 us (1%)
    pallas_call x1, Pallas kernels, make_sketch(): pl.pallas_call(functools.partial(sketch_kernel, size), out_shape=(jax.Sha...  52.2 us
    pallas_call x1, Pallas kernels, project(): pl.pallas_call(functools.partial(project_kernel, size), out_shape=jax.Sha...  40.6 us
    another operation x3, other arithmetic, per_device(): factor_low = jnp.linalg.cholesky(gram)  12.4 us
    another operation x2, other arithmetic, per_device(): lax.linalg.triangular_solve(factor_low, jnp.eye(rank, dtype=F32), left_si...  10.5 us
    unnamed x6, local copies, waits for them, and re-layouts  3.15 us
    convert_element_type x1, other arithmetic, filter_table(): (wiener * (twice[:, None] * twice[None, :] / float(length * length))).ast...  2.51 us

profile of v3, /device:TPU:0, one launch (start us, length us, event | category | flops | bytes accessed | tf_op | source)
XLA Modules:
  0.0 124.7 jit_solution(721905288577960284)
XLA Ops:
  1.3 0.7 broadcast_multiply_fusion
  2.0 0.2 multiply_cosine_fusion
  2.2 0.1 multiply_multiply_fusion
  2.2 0.3 select_convert_fusion
  2.6 0.1 copy.7.pair_t_ref
  2.7 2.5 %multiply_convert_fusion.filters = bf16[64,128,128]{2,1,0:T(8,128)(2,1)S(1)} fusion(f32[128,128]{1,0:T(8,128)S(1)} %multiply_multiply_fusion, f32[64,128]{1,0:T(8,128)S(1)} %get-tuple-element.7, f32[64,128]{1,0:T(8,128)S(1)} %get-tuple-element.15, f32[64,128]{1,0:T(8,128)S(1)} %get-tuple-element.8, f32[64,128]{1,0:T(8,128)S(1)} %get-tuple-element.14), kind=kLoop, calls=%fused_computation | loop fusion | flops 11534336 | bytes 2293760 | tf_op jit(solution)/shard_map/convert_element_type | solution.py:37
  5.2 0.0 copy-start
  5.2 0.9 copy-done
  6.2 0.0 copy-start.1
  6.2 0.7 copy-done.1
  6.8 52.2 %sketch.1 = (bf16[128,256,128]{2,1,0:T(8,128)(2,1)}, f32[256,128]{1,0:T(8,128)S(1)}, f32[128,128]{1,0:T(8,128)S(1)}) custom-call(s32[256]{0:T(256)S(1)} %copy-done.1, s32[1]{0:T(128)S(6)} %copy.13.live_ref, bf16[256,128,128]{2,1,0:T(8,128)(2,1)} %image_ref.1, bf16[1024,128]{1,0:T(8,128)(2,1)S(1)} %copy-done, ...), custom_call_target="tpu_custom_call" | custom-call | tf_op jit(solution)/shard_map/sketch/pallas_call | solution.py:319
  59.1 0.1 copy.8
  59.2 11.7 %cholesky.14 = f32[128,128]{1,0:T(8,128)S(1)} custom-call(f32[128,128]{1,0:T(8,128)S(1)} %fusion.9), custom_call_target="Cholesky" | custom-call | tf_op jit(solution)/shard_map/jit(cholesky)/cholesky | solution.py:455
  70.9 0.6 compare_reduce_fusion
  71.6 0.7 fusion.3
  72.2 9.8 %custom-call.6 = f32[1,128,128]{1,2,0:T(8,128)S(1)} custom-call(f32[1,128,128]{2,1,0:T(8,128)S(1)} %fusion.3), custom_call_target="InvertDiagBlocksLowerTriangular" | custom-call | tf_op jit(solution)/shard_map/triangular_solve | solution.py:457
  82.0 0.2 fusion.7
  82.2 0.3 convolution_convert_fusion
  82.5 40.6 %project.1 = f32[1024,128]{1,0:T(8,128)S(1)} custom-call(bf16[128,256]{1,0:T(8,128)(2,1)S(1)} %bitcast.14, bf16[128,256,128]{2,1,0:T(8,128)(2,1)} %get-tuple-element.11.column_ref), custom_call_target="tpu_custom_call" | custom-call | tf_op jit(solution)/shard_map/project/pallas_call | solution.py:432
  123.1 0.7 copy.10
  123.9 0.8 copy.14
  (7 shorter events, 0.1 us)
Async XLA Ops:
  5.2 1.0 copy-start
  6.2 0.7 copy-start.1

commit v4 on v3

--- a/solution.py
+++ b/solution.py
@@ -364,6 +364,54 @@
     )
 
 
+def basis_kernel(factor_ref, sketch_ref, out_ref, turned_ref):
+    rank = factor_ref.shape[0]
+    row = lax.broadcasted_iota(jnp.int32, (rank, rank), 0)
+    col = lax.broadcasted_iota(jnp.int32, (rank, rank), 1)
+    factor = factor_ref[...]
+    on_diagonal = jnp.where(row == col, factor, 0.0)
+    lower = jnp.where(row > col, factor, 0.0) / jnp.sum(on_diagonal, axis=1, keepdims=True)
+
+    def times(left, right):
+        return jnp.dot(left, right, precision=HIGHEST, preferred_element_type=F32)
+
+    def same_block(shift):
+        return lax.shift_right_logical(row, shift) == lax.shift_right_logical(col, shift)
+
+    shift = 3
+    within = jnp.where(same_block(shift), lower, 0.0)
+    unit = jnp.where(row == col, 1.0, 0.0).astype(F32)
+    square = times(within, within)
+    fourth = times(square, square)
+    inverse = times(times(unit - within, unit + square), unit + fourth)
+    while 1 << shift < rank:
+        off = jnp.where(same_block(shift + 1) & ~same_block(shift), lower, 0.0)
+        inverse = inverse - times(inverse, times(off, inverse))
+        shift += 1
+    inverse = inverse / jnp.sum(on_diagonal, axis=0, keepdims=True)
+    basis = lax.dot_general(
+        sketch_ref[...],
+        inverse,
+        (((1,), (1,)), ((), ())),
+        precision=HIGHEST,
+        preferred_element_type=F32,
+    )
+    out_ref[...] = basis.astype(BF16)
+    turned_ref[...] = basis.T.astype(BF16)
+
+
+def make_basis(factor_low, sketch):
+    slots, rank = sketch.shape
+    return pl.pallas_call(
+        basis_kernel,
+        out_shape=(
+            jax.ShapeDtypeStruct((slots, rank), BF16),
+            jax.ShapeDtypeStruct((rank, slots), BF16),
+        ),
+        name="basis",
+    )(factor_low, sketch)
+
+
 def project_kernel(size, basis_ref, column_ref, out_ref, held, arrived, send_sem, recv_sem):
     me = lax.axis_index("pix")
     length = column_ref.shape[0]
@@ -389,45 +437,53 @@
 
     greet(me, [1 << shift for shift in range(bits_of(size))])
     first = orders[0][0]
-    order = masks_of([first] + orders[0][1:])
-    for mask in order:
-        start = partner_of(me, mask) * rows
+
+    def compute(half, mask):
+        start = partner_of(me, mask) * rows + half * part
+        right = jnp.concatenate([column_ref[start + row] for row in range(part)], axis=1)
+        held[half, mask] = jnp.dot(
+            basis_ref[...], right, preferred_element_type=F32
+        ).astype(BF16)
+
+    def add(half, stage, mask):
+        later = orders[half][stage + 1 :]
+        copy_of(half, stage, mask).wait_recv()
+        total = (
+            held[half, mask].astype(F32)
+            + arrived[half, slots[half, stage, mask]].astype(F32)
+        )
+        if later:
+            held[half, mask] = total.astype(BF16)
+            if mask & later[0]:
+                copy_of(half, stage + 1, mask - later[0]).start()
+        else:
+            height = out_ref.shape[0] // 2
+            out_ref[half * height : (half + 1) * height, :] = total.T
+
+    kept = [masks_of(orders[half][1:]) for half in range(2)]
+    for place in range(len(kept[0]) + 1):
         for half in range(2):
-            right = jnp.concatenate(
-                [column_ref[start + half * part + row] for row in range(part)], axis=1
-            )
-            held[half, mask] = jnp.dot(
-                basis_ref[...], right, preferred_element_type=F32
-            ).astype(BF16)
-            if mask & first:
-                copy_of(half, 0, mask - first).start()
-
-    for stage in range(bits_of(size)):
+            if place < len(kept[0]):
+                mask = kept[half][place]
+                compute(half, first | mask)
+                copy_of(half, 0, mask).start()
+                compute(half, mask)
         for half in range(2):
-            later = orders[half][stage + 1 :]
-            for mask in masks_of(later):
-                copy_of(half, stage, mask).wait_recv()
-                total = (
-                    held[half, mask].astype(F32)
-                    + arrived[half, slots[half, stage, mask]].astype(F32)
-                )
-                if later:
-                    held[half, mask] = total.astype(BF16)
-                    if mask & later[0]:
-                        copy_of(half, stage + 1, mask - later[0]).start()
-                else:
-                    turned = total.T
-                    height = out_ref.shape[0] // 2
-                    out_ref[half * height : (half + 1) * height, :] = turned
+            if place > 0:
+                add(half, 0, kept[half][place - 1])
+    for stage in range(1, bits_of(size)):
+        for place in range(len(masks_of(orders[0][stage + 1 :]))):
+            for half in range(2):
+                add(half, stage, masks_of(orders[half][stage + 1 :])[place])
     for half in range(2):
         for stage in range(bits_of(size)):
             for mask in masks_of(orders[half][stage + 1 :]):
                 copy_of(half, stage, mask).wait_send()
 
 
-def project(columns, basis, size):
+def project(columns, basis_t, size):
     length, slots, _ = columns.shape
-    rank = basis.shape[1]
+    rank = basis_t.shape[0]
     width = length * length // size
     return pl.pallas_call(
         functools.partial(project_kernel, size),
@@ -444,7 +500,7 @@
             collective_id=1, has_side_effects=True, vmem_limit_bytes=48 << 20
         ),
         name="project",
-    )(basis.T, columns)
+    )(basis_t, columns)
 
 
 def per_device(particle_images, defocus_group, live_counts, defocus_values, test_matrix):
@@ -453,12 +509,8 @@
         particle_images, defocus_group, live_counts, defocus_values, test_matrix, size
     )
     factor_low = jnp.linalg.cholesky(gram)
-    rank = gram.shape[0]
-    inverse_t = lax.linalg.triangular_solve(
-        factor_low, jnp.eye(rank, dtype=F32), left_side=False, lower=True, transpose_a=True
-    )
-    range_basis = jnp.dot(sketch, inverse_t, precision=HIGHEST).astype(BF16)
-    return (range_basis, project(columns, range_basis, size))
+    range_basis, basis_t = make_basis(factor_low, sketch)
+    return (range_basis, project(columns, basis_t, size))
 
 
 def solution(mesh):

time: 125 us -> 116 us (0.928)
  other arithmetic: 26.6 us -> 17.5 us
    another operation x2 -> x0, other arithmetic: 10.5 us -> none  [per_device(): lax.linalg.triangular_solve(factor_low, jnp.eye(rank, dtype=F32), left_si...]
    pallas_call x0 -> x1, Pallas kernels: none -> 4.45 us  [make_basis(): pl.pallas_call(basis_kernel, out_shape=(jax.ShapeDtypeStruct((slots, rank...]
    pallas_call x1, Pallas kernels: 40.6 us -> 36.4 us  [project(): pl.pallas_call(functools.partial(project_kernel, size), out_shape=jax.Sha...]
    select_n x0 -> x1, other arithmetic: none -> 1.29 us  [per_device(): factor_low = jnp.linalg.cholesky(gram)]
    unnamed x6 -> x9, local copies, waits for them, and re-layouts: 3.15 us -> 3.91 us
where the time goes in v4:
time: 116 us
  Pallas kernels  93 us (80%)
  other arithmetic  17.5 us (15%)
  local copies, waits for them, and re-layouts  4.09 us (4%)
  between operations  1.39 us (1%)
    pallas_call x1, Pallas kernels, make_sketch(): pl.pallas_call(functools.partial(sketch_kernel, size), out_shape=(jax.Sha...  52.2 us
    pallas_call x1, Pallas kernels, project(): pl.pallas_call(functools.partial(project_kernel, size), out_shape=jax.Sha...  36.4 us
    another operation x3, other arithmetic, per_device(): factor_low = jnp.linalg.cholesky(gram)  12.4 us
    pallas_call x1, Pallas kernels, make_basis(): pl.pallas_call(basis_kernel, out_shape=(jax.ShapeDtypeStruct((slots, rank...  4.45 us
    unnamed x9, local copies, waits for them, and re-layouts  3.91 us
    convert_element_type x1, other arithmetic, filter_table(): (wiener * (twice[:, None] * twice[None, :] / float(length * length))).ast...  2.51 us

profile of v4, /device:TPU:0, one launch (start us, length us, event | category | flops | bytes accessed | tf_op | source)
XLA Modules:
  0.0 116.0 jit_solution(16028077782928951253)
XLA Ops:
  1.3 0.7 broadcast_multiply_fusion
  2.0 0.2 multiply_cosine_fusion
  2.2 0.1 multiply_multiply_fusion
  2.2 0.3 select_convert_fusion
  2.6 0.1 copy.7.pair_t_ref
  2.7 2.5 %multiply_convert_fusion.filters = bf16[64,128,128]{2,1,0:T(8,128)(2,1)S(1)} fusion(f32[128,128]{1,0:T(8,128)S(1)} %multiply_multiply_fusion, f32[64,128]{1,0:T(8,128)S(1)} %get-tuple-element.9, f32[64,128]{1,0:T(8,128)S(1)} %get-tuple-element.17, f32[64,128]{1,0:T(8,128)S(1)} %get-tuple-element.10, f32[64,128]{1,0:T(8,128)S(1)} %get-tuple-element.16), kind=kLoop, calls=%fused_computation | loop fusion | flops 11534336 | bytes 2293760 | tf_op jit(solution)/shard_map/convert_element_type | solution.py:37
  5.2 0.0 copy-start
  5.2 0.9 copy-done
  6.2 0.0 copy-start.3
  6.2 0.7 copy-done.3
  6.8 52.2 %sketch.1 = (bf16[128,256,128]{2,1,0:T(8,128)(2,1)}, f32[256,128]{1,0:T(8,128)S(1)}, f32[128,128]{1,0:T(8,128)S(1)}) custom-call(s32[256]{0:T(256)S(1)} %copy-done.3, s32[1]{0:T(128)S(6)} %copy.10.live_ref, bf16[256,128,128]{2,1,0:T(8,128)(2,1)} %image_ref.1, bf16[1024,128]{1,0:T(8,128)(2,1)S(1)} %copy-done, ...), custom_call_target="tpu_custom_call" | custom-call | tf_op jit(solution)/shard_map/sketch/pallas_call | solution.py:319
  59.1 0.0 copy-start.1
  59.1 0.6 copy-done.1
  59.7 0.1 copy.8
  59.8 11.7 %cholesky.32 = f32[128,128]{1,0:T(8,128)S(1)} custom-call(f32[128,128]{1,0:T(8,128)S(1)} %fusion.6), custom_call_target="Cholesky" | custom-call | tf_op jit(solution)/shard_map/jit(cholesky)/cholesky | solution.py:511
  71.6 0.6 compare_reduce_fusion
  72.2 1.3 %select_select_fusion.factor_ref = f32[128,128]{1,0:T(8,128)} fusion(f32[128,128]{1,0:T(8,128)S(1)} %cholesky.32, pred[]{:T(512)} %compare_reduce_fusion), kind=kLoop, calls=%fused_computation.15 | loop fusion | flops 49152 | bytes 131073 | tf_op jit(solution)/shard_map/jit(cholesky)/select_n | solution.py:511
  73.5 4.4 %basis.1 = (bf16[256,128]{1,0:T(8,128)(2,1)}, bf16[128,256]{1,0:T(8,128)(2,1)}) custom-call(f32[128,128]{1,0:T(8,128)} %select_select_fusion.factor_ref, f32[256,128]{1,0:T(8,128)} %copy-done.1), custom_call_target="tpu_custom_call" | custom-call | tf_op jit(solution)/shard_map/basis/pallas_call | solution.py:405
  78.0 0.0 copy-start.2
  78.0 0.8 copy-done.2
  78.8 36.4 %project.1 = f32[1024,128]{1,0:T(8,128)S(1)} custom-call(bf16[128,256]{1,0:T(8,128)(2,1)S(1)} %copy-done.2, bf16[128,256,128]{2,1,0:T(8,128)(2,1)} %get-tuple-element.15.column_ref), custom_call_target="tpu_custom_call" | custom-call | tf_op jit(solution)/shard_map/project/pallas_call | solution.py:488
  115.2 0.8 copy.11
  (7 shorter events, 0.1 us)
Async XLA Ops:
  5.2 1.0 copy-start
  6.2 0.7 copy-start.3
  59.1 0.7 copy-start.1
  78.0 0.8 copy-start.2
